TPU v7x, 128 devices: a whole 4x4x4 slice. The times are simulated.
128 devices in a mesh: frame: 32 (over y, x, core), tile: 4 (over z).
Axes of the slice: x: 4, y: 4, z: 4, core: 2. Of those that a mesh axis runs over, the one named last changes fastest.
Arguments:
- counts: float32 [1024, 524288], P('frame', 'tile'), may hold values from -1 to 23
- dark_level: float32 [524288], P('tile'), may hold values from 0 to 2
- flat_field: float32 [524288], P('tile'), may hold values from 0.5 to 2
- valid_pixel: int32 [524288], P('tile'), may hold values 0 or 1
- cycle_label: int32 [524288], P('tile'), may hold values from 0 to 32, as said below
- cycle_order: int32 [4, 32, 32], P('tile'), may hold values from 0 to 1024, as said below
- age_bin: int32 [1024], replicated, may hold values from 0 to 15, never falling along the last dimension, each value on 1 to 128 neighbouring positions
Outputs:
- two_time: float32 [32, 1024, 1024], P('frame', 'tile')
- aged_correlation: float32 [32, 16, 1024], P('frame', None, 'tile')
- mean_image: float32 [4, 32, 4096], P('tile', 'frame')
Inputs may be any that keep to these rules, and one draw needn't show every extreme that they name: cycle_order[t, q, :] lists distinct pixel blocks of module t (indices within the module) whose nominal cycle is q, then 131072 // 128 in the unused entries; no block is listed twice in a module; some cycle fills all entries of each module. `cycle_label`: most pixels carry the nominal cycle of the block under which cycle_order lists them.
All inputs are finite; a program needn't handle non-finite values. No bound on the sum of `valid_pixel` on one device may be relied on, other than what follows from the above.
Results may differ from a plain program's by a relative error of at most 0.0003.
Values may be sent and summed in bfloat16 or wider, within the bound.
A program may use at most 128 MiB of HBM per device.

v0:
```python
import jax
import jax.numpy as jnp
from jax import lax
from jax.sharding import PartitionSpec as P

BLK = 128
NA = 16


def band_rows(cmap_rows, age_bin):
    cycle_count, row_count, col_width = cmap_rows.shape
    padded_map = jnp.concatenate([cmap_rows, jnp.zeros_like(cmap_rows)], axis=2)
    span = col_width + row_count
    flattened = jnp.concatenate(
        [
            padded_map.reshape(cycle_count, row_count * span),
            jnp.zeros((cycle_count, row_count), jnp.float32),
        ],
        axis=1,
    )
    skewed_map = flattened.reshape(cycle_count, row_count, span + 1)[:, :, :col_width]
    onehot = (age_bin[None, :] == jnp.arange(NA, dtype=jnp.int32)[:, None]).astype(jnp.float32)
    return jnp.einsum("bi,rid->rbd", onehot, skewed_map, precision=lax.Precision.HIGHEST)


def lag_counts(age_bin, lag_start, lag_count):
    frames = age_bin.shape[0]
    lag_values = lag_start + jnp.arange(lag_count, dtype=jnp.int32)
    inside = (jnp.arange(frames, dtype=jnp.int32)[:, None] + lag_values[None, :] < frames).astype(
        jnp.float32
    )
    onehot = (age_bin[None, :] == jnp.arange(NA, dtype=jnp.int32)[:, None]).astype(jnp.float32)
    return jnp.dot(onehot, inside, precision=lax.Precision.HIGHEST)


def gram_block(frame_block, exchanged):
    return jnp.einsum("irp,jrp->irj", frame_block, exchanged, preferred_element_type=jnp.float32)


def block_rows(values, block_ids, block_total):
    return jnp.take(values.reshape(block_total, BLK), block_ids, axis=0)


def local(counts, dark_level, flat_field, valid_pixel, cycle_label, cycle_order, age_bin):
    pix_module = dark_level.shape[0]
    block_total = pix_module // BLK
    block_order = cycle_order[0]
    cycle_total, block_count = block_order.shape
    slot = block_count * BLK
    frame_part = counts.shape[0]
    is_padding = (block_order >= block_total)[:, :, None]
    block_ids = jnp.where(block_order >= block_total, 0, block_order).reshape(-1)
    cycle_ids = jnp.arange(cycle_total, dtype=jnp.int32)[:, None, None]
    usable = (
        block_rows(valid_pixel, block_ids, block_total)
        .reshape(cycle_total, block_count, BLK)
        .astype(jnp.float32)
    )
    matching = (
        block_rows(cycle_label, block_ids, block_total).reshape(cycle_total, block_count, BLK)
        == cycle_ids
    ).astype(jnp.float32)
    member_blocks = jnp.where(is_padding, 0.0, usable * matching)
    member = member_blocks.reshape(cycle_total, slot)
    slot_gain = block_rows(flat_field, block_ids, block_total) * member_blocks.reshape(
        cycle_total * block_count, BLK
    )
    slot_dark = block_rows(dark_level, block_ids, block_total)
    columns = jnp.take(counts.reshape(frame_part, block_total, BLK), block_ids, axis=1)
    sorted_frames = (
        ((columns - slot_dark[None]) * slot_gain[None])
        .astype(jnp.bfloat16)
        .reshape(frame_part, cycle_total, slot)
    )
    exchanged = lax.all_to_all(sorted_frames, "frame", split_axis=1, concat_axis=0, tiled=True)
    frames = exchanged.shape[0]
    cycle_count = exchanged.shape[1]
    first_cycle = lax.axis_index("frame") * cycle_count
    own_member = lax.dynamic_slice_in_dim(member, first_cycle, cycle_count, 0)
    widened = exchanged.astype(jnp.float32)
    cycle_sums = jnp.transpose(jnp.sum(widened, axis=2), (1, 0))
    image = jnp.sum(widened, axis=0) / frames
    totals, pixel_sums = lax.psum((cycle_sums, jnp.sum(own_member, axis=1)), "tile")
    pixel_total = jnp.maximum(pixel_sums, 1.0)
    clamped = jnp.maximum(totals / pixel_total[:, None], 1.0)
    row_count = frames // lax.axis_size("tile")
    row_start = lax.axis_index("tile") * row_count
    gram_part = lax.psum_scatter(
        gram_block(exchanged, exchanged), "tile", scatter_dimension=0, tiled=True
    )
    row_clamped = lax.dynamic_slice_in_dim(clamped, row_start, row_count, 1)
    two_time = jnp.transpose(gram_part, (1, 0, 2)) / (
        pixel_total[:, None, None] * row_clamped[:, :, None] * clamped[:, None, :]
    )
    lag_total = jnp.maximum(lag_counts(age_bin, row_start, row_count), 1.0)
    whole_map = lax.all_gather(two_time, "tile", axis=1, tiled=True)
    band_sum = lax.dynamic_slice_in_dim(band_rows(whole_map, age_bin), row_start, row_count, 2)
    return (two_time, band_sum / lag_total[None], image[None])


def solution(mesh):
    in_specs = (
        P("frame", "tile"),
        P("tile"),
        P("tile"),
        P("tile"),
        P("tile"),
        P("tile", None, None),
        P(),
    )
    out_specs = (P("frame", "tile", None), P("frame", None, "tile"), P("tile", "frame", None))
    return jax.shard_map(local, mesh=mesh, in_specs=in_specs, out_specs=out_specs, check_vma=False)
```

profile of v0, /device:TPU:18, one launch (start us, length us, event | category | flops | bytes accessed | tf_op | source)
XLA Modules:
  0.0 455.6 jit_solution(15316091511293030886)
XLA Ops:
  7.2 0.0 copy-start
  7.2 0.0 reduce-scatter.2.cloned.1.call-start
  7.2 0.8 squeeze.8
  8.1 0.8 squeeze.9
  8.9 0.7 bitcast_compare_fusion
  9.6 11.8 %copy_bitcast_fusion = f32[32,1024,128]{2,0,1:T(8,128)} fusion(f32[32,131072]{1,0:T(8,128)} %param.11), kind=kLoop, calls=%fused_computation.7 | loop fusion | bytes 33554432 | tf_op jit(solution)/shard_map/reshape | solution.py:69
  21.4 18.1 %gather_fusion = f32[1024,32,128]{2,1,0:T(8,128)} fusion(f32[32,1024,128]{2,0,1:T(8,128)} %copy_bitcast_fusion, s32[1024]{0:T(1024)S(1)} %broadcast_clamp_fusion), kind=kCustom, calls=%fused_computation.4 | custom fusion | bytes 33558528 | tf_op jit(solution)/shard_map/jit(_take)/gather | solution.py:69
  39.6 14.1 %copy.25 = f32[32,1024,128]{2,1,0:T(8,128)} copy(f32[32,1024,128]{2,0,1:T(8,128)} %bitcast.63) | data formatting | bytes 33554432 | tf_op jit(solution)/shard_map/jit(_take)/gather | solution.py:69
  53.7 18.3 %gather.13 = f32[32,32,4096]{2,1,0:T(8,128)} reshape(f32[32,1024,128]{2,1,0:T(8,128)} %copy.25) | data formatting | bytes 33554432 | tf_op jit(solution)/shard_map/jit(_take)/gather | solution.py:69
  72.0 2.8 gather_fusion.1
  74.8 2.8 gather_fusion.4
  77.6 0.1 eq.39
  77.7 2.8 gather_fusion.3
  80.5 2.8 gather_fusion.2
  83.4 0.9 broadcast_select_fusion.1
  84.3 0.1 mul.65
  84.4 0.1 sub.11
  84.5 0.2 broadcast_in_dim.79
  84.7 0.1 copy.41
  84.8 9.5 %multiply_convert_fusion = bf16[32,32,4096]{2,1,0:T(8,128)(2,1)} fusion(f32[32,32,4096]{2,1,0:T(8,128)} %gather.13, f32[32,4096]{1,0:T(8,128)S(1)} %mul.65, f32[32,4096]{1,0:T(8,128)S(1)} %sub.11, pred[32,4096]{1,0:T(8,128)(4,1)S(1)} %bitcast.69), kind=kLoop, calls=%fused_computation.8 | loop fusion | flops 16777216 | bytes 26345472 | tf_op jit(solution)/shard_map/convert_element_type | solution.py:72
  94.2 11.2 %copy.26 = bf16[32,32,4096]{2,0,1:T(8,128)(2,1)} copy(bf16[32,32,4096]{2,1,0:T(8,128)(2,1)} %multiply_convert_fusion) | data formatting | bytes 16777216 | tf_op jit(solution)/shard_map/convert_element_type | solution.py:72
  105.4 99.8 %all_to_all.15 = bf16[32,32,4096]{2,0,1:T(8,128)(2,1)S(1)} all-to-all(bf16[32,32,4096]{2,0,1:T(8,128)(2,1)} %copy.26), channel_id=1, replica_groups=mesh['frame'=32,'tile'=4] {'frame'}, dimensions={1} | all-to-all | bytes 16777216 | tf_op jit(solution)/shard_map/all_to_all | solution.py:75
  205.2 3.2 copy-done.2
  208.5 10.4 %convolution_bitcast_fusion = f32[1024,1,1024]{0,2,1:T(8,128)} fusion(bf16[1024,4096]{1,0:T(8,128)(2,1)S(1)} %bitcast.65), kind=kOutput, calls=%fused_computation.13 | convolution fusion | flops 8589934592 | bytes 12582912 | tf_op jit(solution)/shard_map/irp,jrp->irj/dot_general | solution.py:37
  218.9 0.0 reduce-scatter.2.cloned.1.call-update
  218.9 0.0 all-gather.2.cloned.1.call-start
  218.9 0.2 broadcast_select_fusion
  219.2 0.1 convert_element_type.25
  219.3 0.1 reshape.229
  219.4 0.2 broadcast_in_dim.87
  219.6 0.1 copy.40
  219.7 0.7 fusion.7
  220.3 7.8 %convert_reduce_fusion = (f32[4096]{0:T(1024)S(1)}, f32[32,32]{1,0:T(8,128)S(1)}) fusion(bf16[32,32,4096]{2,0,1:T(8,128)(2,1)} %copy-done.2), kind=kLoop, calls=%fused_computation.5 | loop fusion | flops 12577792 | bytes 8409088 | tf_op jit(solution)/shard_map/reduce_sum | solution.py:82
  228.2 0.1 transpose.25
  228.3 13.4 %all-reduce.2 = (f32[1,1024]{1,0:T(1,128)S(1)}, f32[1]{0:T(128)}) all-reduce(f32[1,1024]{1,0:T(1,128)S(1)} %transpose.25, f32[1]{0:T(128)} %bitcast.13), channel_id=1, replica_groups=mesh['frame'=32,'tile'=4] {'tile'}, use_global_device_ids=true, to_apply=%region_4.7 | all-reduce | flops 1025 | bytes 8200 | tf_op jit(solution)/shard_map/psum | solution.py:83
  242.3 26.0 %reduce-scatter.2.cloned.1.call-done = f32[256,1,1024]{0,2,1:T(8,128)} async-done(((f32[1024,1,1024]{0,2,1:T(8,128)}), f32[256,1,1024]{0,2,1:T(8,128)}) %reduce-scatter.2.cloned.1.call-update) | async-done | bytes 1048592 | tf_op jit(solution)/shard_map/reduce_scatter | solution.py:88
  268.4 2.4 bitcast_divide_fusion
  270.7 0.0 all-gather.2.cloned.1.call-update
  270.8 0.6 broadcast_multiply_fusion
  271.4 2.5 copy.30
  273.9 44.8 %all-gather.2.cloned.1.call-done = f32[1,1024,1024]{1,2,0:T(8,128)} async-done(((f32[1,256,1024]{1,2,0:T(8,128)}), f32[1,1024,1024]{1,2,0:T(8,128)}) %all-gather.2.cloned.1.call-update) | async-done | bytes 4194320 | tf_op jit(solution)/shard_map/all_gather | solution.py:96
  318.7 5.4 %copy.32 = f32[1,1024,1024]{2,1,0:T(8,128)} copy(f32[1,1024,1024]{1,2,0:T(8,128)} %all-gather.2.cloned.1.call-done) | data formatting | bytes 8388608
  324.1 3.3 pad_bitcast_fusion
  327.4 12.5 %copy.36 = f32[1,1,1024,2048]{3,1,2,0:T(1,128)} copy(f32[1,1,1024,2048]{3,2,1,0:T(8,128)S(1)} %pad_bitcast_fusion) | data formatting | bytes 16777216
  339.9 91.3 %pad_reduce_fusion = f32[2098176]{0:T(1024)} fusion(f32[1,2097152]{1,0:T(1,128)} %bitcast.64), kind=kLoop, calls=%fused_computation.9 | loop fusion | bytes 16781312 | tf_op jit(solution)/shard_map/concatenate | solution.py:14
  431.2 12.9 %reshape.231 = f32[1,1024,2049]{2,1,0:T(8,128)} reshape(f32[2098176]{0:T(1024)} %pad_reduce_fusion) | data formatting | bytes 16785408 | tf_op jit(solution)/shard_map/reshape | solution.py:21
  444.1 3.6 fusion
  447.8 0.9 fusion.2
  (20 shorter events, 0.1 us)
Async XLA Ops:
  7.2 64.8 %copy-start = (f32[131072]{0:T(1024)S(1)}, f32[131072]{0:T(1024)}, u32[]{:S(2)}) copy-start(f32[131072]{0:T(1024)} %param.12) | copy-start | bytes 1572868
  7.2 261.2 %reduce-scatter.2.cloned.1.call-start = ((), (), s32[]{:S(2)}) async-start(), calls=%async_computation.2 | async-start | bytes 5242880 | tf_op jit(solution)/shard_map/reduce_scatter | solution.py:88
  53.7 21.1 %copy-start.3 = (s32[131072]{0:T(1024)S(1)}, s32[131072]{0:T(1024)}, u32[]{:S(2)}) copy-start(s32[131072]{0:T(1024)} %param.14) | copy-start | bytes 1572868
  72.0 5.7 %copy-start.4 = (s32[131072]{0:T(1024)S(1)}, s32[131072]{0:T(1024)}, u32[]{:S(2)}) copy-start(s32[131072]{0:T(1024)} %param.15) | copy-start | bytes 1572868
  72.0 8.6 %copy-start.5 = (f32[131072]{0:T(1024)S(1)}, f32[131072]{0:T(1024)}, u32[]{:S(2)}) copy-start(f32[131072]{0:T(1024)} %param.13) | copy-start | bytes 1572868
  205.2 3.2 copy-start.2
  218.9 99.8 %all-gather.2.cloned.1.call-start = ((), (), s32[]{:S(2)}) async-start(), calls=%async_computation.3 | async-start | bytes 5242880 | tf_op jit(solution)/shard_map/all_gather | solution.py:96
  339.9 108.8 %copy-start.1 = (f32[131072]{0:T(1024)S(1)}, f32[131072]{0:T(1024)}, u32[]{:S(2)}) copy-start(f32[131072]{0:T(1024)} %param.12) | copy-start | bytes 1572868
  431.2 12.9 %copy-start.6 = (s32[1024]{0:T(1024)S(1)}, s32[1024]{0:T(1024)}, u32[]{:S(2)}) copy-start(s32[1024]{0:T(1024)} %param.17) | copy-start | bytes 12292
Sparse Core Ops, SparseCore 0:
  219.0 49.2 reduce-scatter.1
  270.9 47.7 all-gather.1
where the time goes:
time: 458 us; the launch traced here: 456 us
  local copies, waits for them, and re-layouts  219 us (48%)
  blocking collectives  113 us (25%)
  waiting for transfers between devices  70.9 us (15%)
  other arithmetic  22.9 us (5%)
  matrix products  15 us (3%)
  between operations  14.9 us (3%)
    all_to_all x1, blocking collectives, local(): lax.all_to_all(sorted_frames, 'frame', split_axis=1, concat_axis=0, tiled...  99.8 us
    concatenate x1, local copies, waits for them, and re-layouts, band_rows(): jnp.concatenate([padded_map.reshape(cycle_count, row_count * span), jnp.z...  91.3 us
    gather x3, local copies, waits for them, and re-layouts, local(): jnp.take(counts.reshape(frame_part, block_total, BLK), block_ids, axis=1)  50.5 us
    all_gather x1, waiting for transfers between devices, local(): whole_map = lax.all_gather(two_time, 'tile', axis=1, tiled=True)  44.8 us
    unnamed x20, local copies, waits for them, and re-layouts  27.1 us
    reduce_scatter x1, waiting for transfers between devices, local(): lax.psum_scatter(gram_block(exchanged, exchanged), 'tile', scatter_dimens...  26 us
    psum x1, blocking collectives, local(): lax.psum((cycle_sums, jnp.sum(own_member, axis=1)), 'tile')  13.4 us
    reshape x1, local copies, waits for them, and re-layouts, band_rows(): flattened.reshape(cycle_count, row_count, span + 1)[:, :, :col_width]  12.9 us
  transfers between devices with their start and end apart: 2, of which 2 were waited for; matrix products, arithmetic and copies ran while one was open for 3% of the time, Pallas kernels for 0%

commit v1 on v0

v1 whole, which is shorter than its diff:
```python
import functools

import jax
import jax.numpy as jnp
from jax import lax
from jax.experimental import pallas as pl
from jax.experimental.pallas import tpu as pltpu
from jax.sharding import PartitionSpec as P

BLK = 128
NA = 16
QSTEP = 4
HALF = 16


def sort_kernel(order, counts, dark, flat, valid, label, out, sums, held, sem):
    c, g = pl.program_id(0), pl.program_id(1)

    def load(i):
        rows = pl.ds(i * HALF, HALF)
        return pltpu.make_async_copy(counts.at[rows, :], held.at[i], sem.at[i])

    @pl.when((c == 0) & (g == 0))
    def _():
        load(0).start()
        load(1).start()
        load(0).wait()

    @pl.when((c == 1) & (g == 0))
    def _():
        load(1).wait()

    block_total = dark.shape[0]
    blocks = order.shape[1]

    @pl.loop(0, QSTEP)
    def _(k):
        q = g * QSTEP + k
        total = jnp.zeros((1, BLK), jnp.float32)
        for b in range(blocks):
            o = order[q, b]
            at = jnp.minimum(o, block_total - 1)
            row = pl.ds(at, 1)
            listed = jnp.where(o < block_total, 1.0, 0.0).astype(jnp.float32)
            usable = jnp.where(label[row, :] == q, valid[row, :].astype(jnp.float32), 0.0) * listed
            total = total + usable
            gain = flat[row, :] * usable
            columns = held[c, :, pl.ds(pl.multiple_of(at * BLK, BLK), BLK)]
            out[k, :, b * BLK : (b + 1) * BLK] = ((columns - dark[row, :]) * gain).astype(jnp.bfloat16)
        sums[k] = total


def sort_frames(block_order, counts, dark, flat, valid, label):
    frames, pixels = counts.shape
    cycles, blocks = block_order.shape
    slot = blocks * BLK
    table = pl.BlockSpec((pixels // BLK, BLK), lambda c, g, order: (0, 0))
    return pl.pallas_call(
        sort_kernel,
        grid_spec=pltpu.PrefetchScalarGridSpec(
            num_scalar_prefetch=1,
            grid=(frames // HALF, cycles // QSTEP),
            in_specs=[pl.BlockSpec(memory_space=pl.ANY), table, table, table, table],
            out_specs=[
                pl.BlockSpec((QSTEP, HALF, slot), lambda c, g, order: (g, c, 0)),
                pl.BlockSpec((QSTEP, 1, BLK), lambda c, g, order: (g, 0, 0)),
            ],
            scratch_shapes=[
                pltpu.VMEM((frames // HALF, HALF, pixels), jnp.float32),
                pltpu.SemaphoreType.DMA((frames // HALF,)),
            ],
        ),
        out_shape=[
            jax.ShapeDtypeStruct((cycles, frames, slot), jnp.bfloat16),
            jax.ShapeDtypeStruct((cycles, 1, BLK), jnp.float32),
        ],
        compiler_params=pltpu.CompilerParams(
            dimension_semantics=("arbitrary", "arbitrary"), vmem_limit_bytes=40 << 20
        ),
        cost_estimate=pl.CostEstimate(flops=3 * frames * cycles * slot, bytes_accessed=24 << 20, transcendentals=0),
    )(block_order, counts, dark, flat, valid, label)


def finish_kernel(gram, scale_col, scale_row, bins, two_time, bands, *, axis):
    rows, width = gram.shape
    cmap = gram[...] / (scale_col[...] * scale_row[...])
    two_time[...] = cmap
    first = lax.axis_index(axis) * rows
    lane = lax.broadcasted_iota(jnp.int32, (8, width), 1)
    sub = lax.broadcasted_iota(jnp.int32, (8, width), 0)
    pieces = []
    for r in range(0, rows, 8):
        part = cmap[r : r + 8, :]
        part = jnp.where(lane >= first + r + sub, part, 0.0)
        part = pltpu.roll(part, lax.rem(width - (first + r), width), 1)
        for bit in (1, 2, 4):
            part = jnp.where((sub & bit) != 0, pltpu.roll(part, width - bit, 1), part)
        pieces.append(part)
    skewed = jnp.concatenate(pieces, axis=0)
    onehot = (bins[...] == lax.broadcasted_iota(jnp.int32, (NA, rows), 0)).astype(jnp.float32)
    bands[...] = jnp.dot(onehot, skewed, precision=lax.Precision.HIGHEST, preferred_element_type=jnp.float32)


def finish(gram, scale_col, scale_row, bins):
    rows, width = gram.shape
    return pl.pallas_call(
        functools.partial(finish_kernel, axis="tile"),
        out_shape=[
            jax.ShapeDtypeStruct((rows, width), jnp.float32),
            jax.ShapeDtypeStruct((NA, width), jnp.float32),
        ],
        in_specs=[pl.BlockSpec(memory_space=pltpu.VMEM)] * 4,
        out_specs=[pl.BlockSpec(memory_space=pltpu.VMEM)] * 2,
        compiler_params=pltpu.CompilerParams(vmem_limit_bytes=32 << 20),
    )(gram, scale_col, scale_row, bins)


def local(counts, dark_level, flat_field, valid_pixel, cycle_label, cycle_order, age_bin):
    block_total = dark_level.shape[0] // BLK
    table = (block_total, BLK)
    sorted_frames, member_sums = sort_frames(
        cycle_order[0],
        counts,
        dark_level.reshape(table),
        flat_field.reshape(table),
        valid_pixel.reshape(table),
        cycle_label.reshape(table),
    )
    exchanged = lax.all_to_all(sorted_frames, "frame", split_axis=0, concat_axis=1, tiled=True)[0]
    frames = exchanged.shape[0]
    own = lax.dynamic_slice_in_dim(member_sums, lax.axis_index("frame"), 1, 0)
    widened = exchanged.astype(jnp.float32)
    cycle_sums = jnp.sum(widened, axis=1)
    image = jnp.sum(widened, axis=0) / frames
    gram = jnp.dot(exchanged, exchanged.T, preferred_element_type=jnp.float32)
    totals, pixels = lax.psum((cycle_sums, jnp.sum(own)), "tile")
    pixel_total = jnp.maximum(pixels, 1.0)
    clamped = jnp.maximum(totals / pixel_total, 1.0)
    row_count = frames // lax.axis_size("tile")
    row_start = lax.axis_index("tile") * row_count
    gram_rows = lax.psum_scatter(gram, "tile", scatter_dimension=0, tiled=True)
    row_scale = pixel_total * lax.dynamic_slice_in_dim(clamped, row_start, row_count, 0)
    bins = lax.dynamic_slice_in_dim(age_bin, row_start, row_count, 0)
    two_time, bands = finish(gram_rows, row_scale[:, None], clamped[None, :], bins[None, :])
    band_sum = lax.psum_scatter(bands, "tile", scatter_dimension=1, tiled=True)
    lags = row_start + jnp.arange(row_count, dtype=jnp.int32)
    label = jnp.arange(NA, dtype=jnp.int32)[:, None]
    below = jnp.sum((age_bin[None, :] < label).astype(jnp.int32), axis=1)
    upto = jnp.sum((age_bin[None, :] <= label).astype(jnp.int32), axis=1)
    count = jnp.minimum(upto[:, None], frames - lags[None, :]) - below[:, None]
    lag_total = jnp.maximum(count, 1).astype(jnp.float32)
    return (two_time[None], (band_sum / lag_total)[None], image[None, None])


def solution(mesh):
    in_specs = (
        P("frame", "tile"),
        P("tile"),
        P("tile"),
        P("tile"),
        P("tile"),
        P("tile", None, None),
        P(),
    )
    out_specs = (P("frame", "tile", None), P("frame", None, "tile"), P("tile", "frame", None))
    return jax.shard_map(local, mesh=mesh, in_specs=in_specs, out_specs=out_specs, check_vma=False)
```

time: 458 us -> 225 us (0.49)
  local copies, waits for them, and re-layouts: 219 us -> 9.6 us
  waiting for transfers between devices: 70.9 us -> 46.4 us
  Pallas kernels: 0 us -> 19.1 us
  other arithmetic: 22.9 us -> 10.7 us
  matrix products: 15 us -> 10.4 us
    concatenate x1 -> x0, local copies, waits for them, and re-layouts: 91.3 us -> none  [band_rows(): jnp.concatenate([padded_map.reshape(cycle_count, row_count * span), jnp.z...]
    gather x7 -> x0, local copies, waits for them, and re-layouts: 61.8 us -> none  [the longest x3 50.5 us: local(): jnp.take(counts.reshape(frame_part, block_total, BLK), block_ids, axis=1)]
    all_gather x1 -> x0, waiting for transfers between devices: 44.8 us -> none  [local(): whole_map = lax.all_gather(two_time, 'tile', axis=1, tiled=True)]
    reshape x3 -> x0, local copies, waits for them, and re-layouts: 24.8 us -> none  [the longest x1 12.9 us: band_rows(): flattened.reshape(cycle_count, row_count, span + 1)[:, :, :col_width]]
    reduce_scatter x1 -> x2, waiting for transfers between devices: 26 us -> 46.3 us  [the longest x1 26.6 us: local(): gram_rows = lax.psum_scatter(gram, 'tile', scatter_dimension=0, tiled=True)]
    pallas_call x0 -> x2, Pallas kernels: none -> 19.1 us  [the longest x1 15.7 us: sort_frames(): pl.pallas_call(sort_kernel, grid_spec=pltpu.PrefetchScalarGridSpec(num_sc...]
    unnamed x20 -> x16, local copies, waits for them, and re-layouts: 27.1 us -> 9.32 us
    convert_element_type x2 -> x0, local copies, waits for them, and re-layouts: 11.3 us -> none  [the longest x1 11.2 us: local(): sorted_frames = ((columns - slot_dark[None]) * slot_gain[None]).astype(jn...]
  transfers between devices with their start and end apart: 2 -> 2, of which waited for: 2 -> 2; matrix products, arithmetic and copies ran while one was open for 3% -> 4% of each run, Pallas kernels for 0% -> 0%
where the time goes in v1:
time: 225 us; the launch traced here: 224 us
  blocking collectives  113 us (50%)
  waiting for transfers between devices  46.4 us (21%)
  Pallas kernels  19.1 us (8%)
  between operations  14.7 us (7%)
  other arithmetic  10.7 us (5%)
  matrix products  10.4 us (5%)
  local copies, waits for them, and re-layouts  9.6 us (4%)
    all_to_all x1, blocking collectives, local(): lax.all_to_all(sorted_frames, 'frame', split_axis=0, concat_axis=1, tiled...  99.6 us
    reduce_scatter x1, waiting for transfers between devices, local(): gram_rows = lax.psum_scatter(gram, 'tile', scatter_dimension=0, tiled=True)  26.6 us
    reduce_scatter x1, waiting for transfers between devices, local(): band_sum = lax.psum_scatter(bands, 'tile', scatter_dimension=1, tiled=True)  19.7 us
    pallas_call x1, Pallas kernels, sort_frames(): pl.pallas_call(sort_kernel, grid_spec=pltpu.PrefetchScalarGridSpec(num_sc...  15.7 us
    psum x1, blocking collectives, local(): totals, pixels = lax.psum((cycle_sums, jnp.sum(own)), 'tile')  13.2 us
    dot_general x1, matrix products, local(): gram = jnp.dot(exchanged, exchanged.T, preferred_element_type=jnp.float32)  10.4 us
    unnamed x16, local copies, waits for them, and re-layouts  9.32 us
    reduce_sum x1, other arithmetic, local(): image = jnp.sum(widened, axis=0) / frames  7.84 us
  transfers between devices with their start and end apart: 2, of which 2 were waited for; matrix products, arithmetic and copies ran while one was open for 4% of the time, Pallas kernels for 0%

profile of v1, /device:TPU:18, one launch (start us, length us, event | category | flops | bytes accessed | tf_op | source)
XLA Modules:
  0.0 223.8 jit_solution(8254457391862531704)
XLA Ops:
  7.2 0.0 reduce-scatter.3.cloned.1.call-start
  7.2 0.0 copy-start.1
  7.2 1.0 copy-done.1
  8.3 0.0 copy-start.2
  8.3 1.0 copy-done.2
  9.3 0.0 copy-start.3
  9.3 1.0 copy-done.3
  10.3 0.0 copy-start.4
  10.3 1.0 copy-done.4
  11.4 0.0 copy-start.5
  11.4 0.7 copy-done.5
  12.1 15.7 %shard_map.94 = (bf16[32,32,4096]{2,1,0:T(8,128)(2,1)S(1)}, f32[32,1,128]{2,1,0:T(1,128)S(1)}) custom-call(s32[32,32]{1,0:T(8,128)S(1)} %bitcast.20, f32[32,131072]{1,0:T(8,128)} %counts.1, f32[1024,128]{1,0:T(8,128)S(1)} %bitcast.15, f32[1024,128]{1,0:T(8,128)S(1)} %bitcast.16, s32[1024,128]{1,0:T(8,128)S(1)} %bitcast.17, s32[1024,128]{1,0:T(8,128)S(1)} %bitcast.18), custom_call_target="tpu_custom_call" | custom-call | flops 12582912 | bytes 25165824 | tf_op jit(solution)/shard_map/pallas_call | solution.py:58
  27.9 99.6 %all_to_all.4 = bf16[32,32,4096]{2,1,0:T(8,128)(2,1)S(1)} all-to-all(bf16[32,32,4096]{2,1,0:T(8,128)(2,1)S(1)} %get-tuple-element.7), channel_id=1, replica_groups=mesh['frame'=32,'tile'=4] {'frame'}, dimensions={0} | all-to-all | bytes 16777216 | tf_op jit(solution)/shard_map/all_to_all | solution.py:129
  127.5 0.0 copy-start.6
  127.5 3.2 %copy-done.6 = bf16[32,32,4096]{2,1,0:T(8,128)(2,1)} copy-done((bf16[32,32,4096]{2,1,0:T(8,128)(2,1)}, bf16[32,32,4096]{2,1,0:T(8,128)(2,1)S(1)}, u32[]{:S(2)}) %copy-start.6) | copy-done | bytes 8388632
  130.7 0.0 copy-start.7
  130.7 10.4 %fusion = f32[1024,1024]{1,0:T(8,128)} fusion(bf16[1024,4096]{1,0:T(8,128)(2,1)S(1)} %bitcast.22), kind=kOutput, calls=%fused_computation.12 | convolution fusion | flops 8589934592 | bytes 12582912 | tf_op jit(solution)/shard_map/dot_general | solution.py:135
  141.1 0.0 reduce-scatter.3.cloned.1.call-update
  141.1 0.0 reduce-scatter.5.cloned.1.call-start
  141.2 0.6 dynamic-slice_reduce_fusion
  141.8 0.0 copy-done.7
  141.8 0.1 dynamic_slice.11
  141.9 0.1 convert_reduce_fusion.3
  142.0 7.8 %convert_reduce_fusion = (f32[4096]{0:T(1024)S(1)}, f32[32,32]{1,0:T(8,128)S(1)}) fusion(bf16[32,32,4096]{2,1,0:T(8,128)(2,1)} %copy-done.6), kind=kLoop, calls=%fused_computation | loop fusion | flops 12577792 | bytes 8409088 | tf_op jit(solution)/shard_map/reduce_sum | solution.py:134
  149.8 0.1 reduce_sum.49
  149.9 13.2 %all-reduce = (f32[1024]{0:T(1024)S(1)}, f32[]{:T(128)}) all-reduce(f32[1024]{0:T(1024)S(1)} %reduce_sum.49, f32[]{:T(128)} %dynamic-slice_reduce_fusion), channel_id=1, replica_groups=mesh['frame'=32,'tile'=4] {'tile'}, use_global_device_ids=true, to_apply=%region_4.0 | all-reduce | flops 1025 | bytes 8200 | tf_op jit(solution)/shard_map/psum | solution.py:136
  163.7 0.1 dynamic-slice_multiply_fusion
  163.8 0.1 copy.11.scale_col
  164.0 26.6 %reduce-scatter.3.cloned.1.call-done.gram = f32[256,1024]{1,0:T(8,128)} async-done(((f32[1024,1024]{1,0:T(8,128)}), f32[256,1024]{1,0:T(8,128)}) %reduce-scatter.3.cloned.1.call-update) | async-done | bytes 1048592 | tf_op jit(solution)/shard_map/reduce_scatter | solution.py:141
  190.6 0.0 copy-start
  190.6 1.2 copy-done
  191.8 3.4 %shard_map.95 = (f32[256,1024]{1,0:T(8,128)}, f32[16,1024]{1,0:T(8,128)}) custom-call(f32[256,1024]{1,0:T(8,128)S(1)} %copy-done, f32[256,1]{1,0:T(8,128)S(1)} %copy.11.scale_col, f32[1,1024]{1,0:T(1,128)S(1)} %bitcast.19, s32[1,256]{1,0:T(1,128)S(1)} %bitcast.21), custom_call_target="tpu_custom_call" | custom-call | tf_op jit(solution)/shard_map/pallas_call | solution.py:106
  195.2 0.0 reduce-scatter.5.cloned.1.call-update
  195.2 0.6 broadcast_multiply_fusion
  195.8 19.7 %reduce-scatter.5.cloned.1.call-done = f32[16,256]{1,0:T(8,128)} async-done(((f32[16,1024]{1,0:T(8,128)}), f32[16,256]{1,0:T(8,128)}) %reduce-scatter.5.cloned.1.call-update) | async-done | bytes 16400 | tf_op jit(solution)/shard_map/reduce_scatter | solution.py:145
  215.5 1.4 divide_bitcast_fusion
  (2 shorter events, 0.0 us)
Async XLA Ops:
  7.2 183.4 %reduce-scatter.3.cloned.1.call-start = ((), (), s32[]{:S(2)}) async-start(), calls=%async_computation.3 | async-start | bytes 5242880 | tf_op jit(solution)/shard_map/reduce_scatter | solution.py:141
  7.2 1.0 copy-start.1
  8.3 1.0 copy-start.2
  9.3 1.0 copy-start.3
  10.3 1.0 copy-start.4
  11.4 0.7 copy-start.5
  127.5 3.2 %copy-start.6 = (bf16[32,32,4096]{2,1,0:T(8,128)(2,1)}, bf16[32,32,4096]{2,1,0:T(8,128)(2,1)S(1)}, u32[]{:S(2)}) copy-start(bf16[32,32,4096]{2,1,0:T(8,128)(2,1)S(1)} %all_to_all.4) | copy-start | bytes 25165828
  130.7 11.1 %copy-start.7 = (s32[1024]{0:T(1024)S(1)}, s32[1024]{0:T(1024)}, u32[]{:S(2)}) copy-start(s32[1024]{0:T(1024)} %param.13) | copy-start | bytes 12292
  141.1 74.4 %reduce-scatter.5.cloned.1.call-start = ((), (), s32[]{:S(2)}) async-start(), calls=%async_computation.4 | async-start | bytes 81920 | tf_op jit(solution)/shard_map/reduce_scatter | solution.py:145
  190.6 1.2 copy-start
Sparse Core Ops, SparseCore 0:
  141.2 49.2 reduce-scatter.2
  195.3 20.1 reduce-scatter.4

commit v2 on v1

v2 whole, which is shorter than its diff:
```python
import jax
import jax.numpy as jnp
from jax import lax
from jax.experimental import pallas as pl
from jax.experimental.pallas import tpu as pltpu
from jax.sharding import PartitionSpec as P

BLK = 128
NA = 16
QSTEP = 4
HALF = 16
MESH = pl.DeviceIdType.MESH


def sort_kernel(order, counts, dark, flat, valid, label, out, sums, held, sem):
    c, g = pl.program_id(0), pl.program_id(1)

    def load(i):
        rows = pl.ds(i * HALF, HALF)
        return pltpu.make_async_copy(counts.at[rows, :], held.at[i], sem.at[i])

    @pl.when((c == 0) & (g == 0))
    def _():
        load(0).start()
        load(1).start()
        load(0).wait()

    @pl.when((c == 1) & (g == 0))
    def _():
        load(1).wait()

    block_total = dark.shape[0]
    blocks = order.shape[1]

    @pl.loop(0, QSTEP)
    def _(k):
        q = g * QSTEP + k
        total = jnp.zeros((1, BLK), jnp.float32)
        for b in range(blocks):
            o = order[q, b]
            at = jnp.minimum(o, block_total - 1)
            row = pl.ds(at, 1)
            listed = jnp.where(o < block_total, 1.0, 0.0).astype(jnp.float32)
            usable = jnp.where(label[row, :] == q, valid[row, :].astype(jnp.float32), 0.0) * listed
            total = total + usable
            gain = flat[row, :] * usable
            columns = held[c, :, pl.ds(pl.multiple_of(at * BLK, BLK), BLK)]
            out[k, :, b * BLK : (b + 1) * BLK] = ((columns - dark[row, :]) * gain).astype(jnp.bfloat16)
        sums[k] = total


def sort_frames(block_order, counts, dark, flat, valid, label):
    frames, pixels = counts.shape
    cycles, blocks = block_order.shape
    slot = blocks * BLK
    table = pl.BlockSpec((pixels // BLK, BLK), lambda c, g, order: (0, 0))
    return pl.pallas_call(
        sort_kernel,
        grid_spec=pltpu.PrefetchScalarGridSpec(
            num_scalar_prefetch=1,
            grid=(frames // HALF, cycles // QSTEP),
            in_specs=[pl.BlockSpec(memory_space=pl.ANY), table, table, table, table],
            out_specs=[
                pl.BlockSpec((QSTEP, HALF, slot), lambda c, g, order: (g, c, 0)),
                pl.BlockSpec((QSTEP, 1, BLK), lambda c, g, order: (g, 0, 0)),
            ],
            scratch_shapes=[
                pltpu.VMEM((frames // HALF, HALF, pixels), jnp.float32),
                pltpu.SemaphoreType.DMA((frames // HALF,)),
            ],
        ),
        out_shape=[
            jax.ShapeDtypeStruct((cycles, frames, slot), jnp.bfloat16),
            jax.ShapeDtypeStruct((cycles, 1, BLK), jnp.float32),
        ],
        compiler_params=pltpu.CompilerParams(
            dimension_semantics=("arbitrary", "arbitrary"), vmem_limit_bytes=40 << 20
        ),
        cost_estimate=pl.CostEstimate(flops=3 * frames * cycles * slot, bytes_accessed=24 << 20, transcendentals=0),
    )(block_order, counts, dark, flat, valid, label)


def steps_of(k, e, h):
    dy = (0, 2)[e] if k < 2 else (1, 3)[e]
    dx = (0, 2)[h] if k % 2 == 0 else (3, 1)[h]
    return dy, dx


def contract(a, b):
    return lax.dot_general(a, b, (((1,), (1,)), ((), ())), preferred_element_type=jnp.float32)


def exchange_kernel(
    frames_in,
    members,
    ages,
    two_time,
    aged,
    image,
    x_all,
    part,
    inbox,
    total,
    shared,
    sums,
    sums_in,
    bands,
    bands_in,
    own_sem,
    xs_sem,
    xr_sem,
    ps_sem,
    pr_sem,
    hs_sem,
    hr_sem,
    ss_sem,
    sr_sem,
    bs_sem,
    br_sem,
):
    f, t = lax.axis_index("frame"), lax.axis_index("tile")
    y, x, c = f // 8, (f // 2) % 4, f % 2
    role = (y - t + 4) % 4
    odd, side = role % 2, role // 2

    def chip(dy, dx, sign):
        return (((y + sign * dy + 4) % 4) * 4 + (x + sign * dx + 4) % 4) * 2

    def tile_of(r):
        return (y - r + 4) % 4

    def frames_of(slot):
        return x_all.at[pl.ds(pl.multiple_of(slot * 32, 32), 32), :]

    def send(k, e, h, dc):
        dy, dx = steps_of(k, e, h)
        dst = chip(dy, dx, 1) + (c + dc) % 2
        m = 4 * k + 2 * e + h
        return pltpu.make_async_remote_copy(
            src_ref=frames_in.at[dst],
            dst_ref=frames_of(2 * m + c),
            send_sem=xs_sem.at[m, dc],
            recv_sem=xr_sem.at[2 * m + c],
            device_id=(dst, t),
            device_id_type=MESH,
        )

    def arrival(k, e, h, dc):
        dy, dx = steps_of(k, e, h)
        sc = (c + dc) % 2
        m = 4 * k + 2 * e + h
        return pltpu.make_async_remote_copy(
            src_ref=frames_in.at[f],
            dst_ref=frames_of(2 * m + sc),
            send_sem=xs_sem.at[m, dc],
            recv_sem=xr_sem.at[2 * m + sc],
            device_id=(chip(dy, dx, -1) + sc, t),
            device_id_type=MESH,
        )

    def quarter():
        return [(e, h, dc) for first in range(2) for dc in range(2) for e, h in ((0, first), (1, 1 - first))]

    def is_own(k, e, h, dc):
        return (k, e, h, dc) == (0, 0, 0, 0)

    barrier = pltpu.get_barrier_semaphore()
    for dy in range(4):
        for dx in range(4):
            for dc in range(2):
                if (dy, dx, dc) != (0, 0, 0):
                    peer = chip(dy, dx, 1) + (c + dc) % 2
                    pl.semaphore_signal(barrier, inc=1, device_id=(peer, t), device_id_type=MESH)
    for dz in range(1, 4):
        pl.semaphore_signal(barrier, inc=1, device_id=(f, (t + dz) % 4), device_id_type=MESH)
    pl.semaphore_wait(barrier, 34)

    own = pltpu.make_async_copy(frames_in.at[f], frames_of(c), own_sem)
    own.start()
    for k in range(2):
        for e, h, dc in quarter():
            if not is_own(k, e, h, dc):
                send(k, e, h, dc).start()

    ones = jnp.ones((8, 1024), jnp.bfloat16)
    width = x_all.shape[1]
    chunks = width // 1024
    group = lambda r, j: 4 * (r % 2) + 2 * j + r // 2

    def tile_copy(src, dst, send_sem, recv_sem, tile):
        return pltpu.make_async_remote_copy(
            src_ref=src, dst_ref=dst, send_sem=send_sem, recv_sem=recv_sem, device_id=(f, tile), device_id_type=MESH
        )

    def partial_copy(k, cg, half):
        tile = tile_of(cg // 2 + 2 * half)
        slot = 3 - (tile - t + 4) % 4
        return tile, lambda: tile_copy(
            part.at[k, cg, half],
            inbox.at[k, cg % 2, slot],
            ps_sem.at[k, cg, half],
            pr_sem.at[k, cg % 2, slot],
            tile,
        )

    def share_copy(k, j, e):
        g = group(role, j)
        return tile_copy(
            total.at[k, j, pl.ds(128 * e, 128), :],
            shared.at[k % 2, g],
            hs_sem.at[k, j, e],
            hr_sem.at[k % 2, g],
            tile_of(k // 2 + 2 * e),
        )

    def shares_to_wait(k, start):
        for j in range(2):
            for e in range(2):
                for p in range(2):
                    if 2 * p + j < k:

                        @pl.when((odd == p) & (role != k // 2 + 2 * e))
                        def _():
                            if start:
                                share_copy(k, j, e).start()
                            else:
                                share_copy(k, j, e).wait_send()

    for k in range(4):
        new = pl.ds(256 * k, 256)
        for e, h, dc in quarter():
            if is_own(k, e, h, dc):
                own.wait()
            else:
                arrival(k, e, h, dc).wait_recv()
        if k < 2:
            for e, h, dc in quarter():
                send(k + 2, e, h, dc).start()
        for cg in range(k + 1):

            def body(i, acc):
                at = pl.ds(pl.multiple_of(i * 1024, 1024), 1024)
                return acc + contract(x_all[new, at], x_all[256 * cg : 256 * cg + 256, at])

            acc = lax.fori_loop(0, chunks, body, jnp.zeros((256, 256), jnp.float32))
            for half in range(2):
                part[k, cg, half] = acc[:, 128 * half : 128 * half + 128]
            for half in range(2):
                tile, copy = partial_copy(k, cg, half)

                @pl.when(tile != t)
                def _():
                    copy().start()

        line = jnp.zeros((8, 256), jnp.float32)
        for i in range(chunks):
            line = line + contract(ones, x_all[new, i * 1024 : (i + 1) * 1024])
        sums[k, :, 0:256] = line
        sums[k, :, 256:384] = jnp.broadcast_to(members[f], (8, 128))
        for dz in range(1, 4):
            tile_copy(
                sums.at[k], sums_in.at[k, 3 - dz], ss_sem.at[k, dz - 1], sr_sem.at[k, 3 - dz], (t + dz) % 4
            ).start()
        for i in range(chunks):
            at = slice(i * 1024, (i + 1) * 1024)
            row = jnp.dot(ones[:, 0:256], x_all[new, at], preferred_element_type=jnp.float32)[0:1]
            if k == 0:
                image[:, at] = row
            elif k < 3:
                image[:, at] = image[:, at] + row
            else:
                image[:, at] = (image[:, at] + row) * (1.0 / 1024.0)

        for j in range(2):
            for p in range(2):
                cg = 2 * p + j
                if cg <= k:

                    @pl.when(odd == p)
                    def _():
                        for slot in range(3):
                            tile_copy(
                                part.at[k, cg, 0], inbox.at[k, j, slot], ps_sem.at[k, cg, 0], pr_sem.at[k, j, slot], (t + slot + 1) % 4
                            ).wait_recv()
                        total[k, j] = (part[k, cg, side] + inbox[k, j, 0]) + (inbox[k, j, 1] + inbox[k, j, 2])
                        if cg < k:
                            for e in range(2):

                                @pl.when(role == k // 2 + 2 * e)
                                def _():
                                    shared[k % 2, group(role, j)] = total[k, j, 128 * e : 128 * e + 128, :]

        shares_to_wait(k, True)

    for k in range(4):
        for slot in range(3):
            tile_copy(
                sums.at[k], sums_in.at[k, slot], ss_sem.at[k, 0], sr_sem.at[k, slot], (t + slot + 1) % 4
            ).wait_recv()
    quarters = [
        (sums[k] + sums_in[k, 0]) + (sums_in[k, 1] + sums_in[k, 2]) for k in range(4)
    ]
    pixel_total = jnp.maximum(jnp.sum(quarters[0][0:1, 256:384], axis=1, keepdims=True), 1.0)
    clamped = [jnp.maximum(qs[:, 0:256] / pixel_total, 1.0) for qs in quarters]
    lane = lax.broadcasted_iota(jnp.int32, (128, 128), 1)
    low = lane < 64

    for p in range(2):

        @pl.when(odd == p)
        def _():
            for jj in range(2):
                kk = 2 * p + jj
                mine = jnp.where(side == 0, clamped[kk][:, 0:128], clamped[kk][:, 128:256])
                row_scale = jnp.transpose(pixel_total * mine)[:, 0:1]

                def block(g):
                    kg, e = g // 2, g % 2
                    if kg < kk:

                        @pl.when(group(role, g // 2 - 2 * (g // 4)) != g)
                        def _():
                            tile_copy(
                                total.at[0, 0, pl.ds(0, 128), :], shared.at[jj, g], hs_sem.at[0, 0, 0], hr_sem.at[jj, g], (t + 1) % 4
                            ).wait_recv()

                        value = shared[jj, g]
                    else:
                        value = jnp.transpose(total[kg, jj, 128 * e : 128 * e + 128, :])
                    return value / (row_scale * clamped[kg][0:1, 128 * e : 128 * e + 128])

                for r in range(4):
                    a = block(4 * (r % 2) + r // 2)
                    b = block(4 * (r % 2) + r // 2 + 2)
                    first = jnp.where(low, a, pltpu.roll(b, 64, 1))
                    second = jnp.where(low, pltpu.roll(a, 64, 1), b)
                    natural = pltpu.roll(jnp.concatenate([first, second], axis=1), 64 * x, 1)
                    at = pl.ds(pl.multiple_of(tile_of(r) * 256, 256), 256)
                    for h in range(2):
                        rows = pl.ds(pl.multiple_of(64 * ((x + jj + 2 * h) % 4), 64), 64)
                        two_time[rows, at] = natural[64 * h : 64 * h + 64, :]

    first = t * 256
    lane8 = lax.broadcasted_iota(jnp.int32, (8, 1024), 1)
    sub8 = lax.broadcasted_iota(jnp.int32, (8, 1024), 0)
    pieces = []
    for r in range(0, 256, 8):
        piece = two_time[r : r + 8, :]
        piece = jnp.where(lane8 >= first + r + sub8, piece, 0.0)
        piece = pltpu.roll(piece, (2048 - (first + r)) % 1024, 1)
        for bit in (1, 2, 4):
            piece = jnp.where((sub8 & bit) != 0, pltpu.roll(piece, 1024 - bit, 1), piece)
        pieces.append(piece)
    skewed = jnp.concatenate(pieces, axis=0)
    bins = ages[:, pl.ds(pl.multiple_of(first, 256), 256)]
    onehot = (bins == lax.broadcasted_iota(jnp.int32, (NA, 256), 0)).astype(jnp.float32)
    band = jnp.dot(onehot, skewed, precision=lax.Precision.HIGHEST, preferred_element_type=jnp.float32)
    for r in range(4):
        bands[r] = band[:, 256 * r : 256 * r + 256]
    label = lax.broadcasted_iota(jnp.int32, (NA, 1024), 0)
    below = jnp.sum((ages[...] < label).astype(jnp.float32), axis=1, keepdims=True)
    upto = jnp.sum((ages[...] <= label).astype(jnp.float32), axis=1, keepdims=True)
    for dz in range(1, 4):
        peer = (t + dz) % 4
        tile_copy(bands.at[peer], bands_in.at[3 - dz], bs_sem.at[dz - 1], br_sem.at[3 - dz], peer).start()
    lags = (first + lax.broadcasted_iota(jnp.int32, (NA, 256), 1)).astype(jnp.float32)
    lag_total = jnp.maximum(jnp.minimum(upto, 1024.0 - lags) - below, 1.0)
    for slot in range(3):
        tile_copy(bands.at[0], bands_in.at[slot], bs_sem.at[0], br_sem.at[slot], (t + slot + 1) % 4).wait_recv()
    aged[...] = ((bands[t] + bands_in[0]) + (bands_in[1] + bands_in[2])) / lag_total

    for k in range(4):
        for e, h, dc in quarter():
            if not is_own(k, e, h, dc):
                send(k, e, h, dc).wait_send()
        for cg in range(k + 1):
            for half in range(2):
                tile, copy = partial_copy(k, cg, half)

                @pl.when(tile != t)
                def _():
                    copy().wait_send()

        for dz in range(1, 4):
            tile_copy(
                sums.at[k], sums_in.at[k, 3 - dz], ss_sem.at[k, dz - 1], sr_sem.at[k, 3 - dz], (t + dz) % 4
            ).wait_send()
        shares_to_wait(k, False)
    for dz in range(1, 4):
        peer = (t + dz) % 4
        tile_copy(bands.at[peer], bands_in.at[3 - dz], bs_sem.at[dz - 1], br_sem.at[3 - dz], peer).wait_send()


def exchange(sorted_frames, members, ages):
    slot = sorted_frames.shape[2]
    vmem = pl.BlockSpec(memory_space=pltpu.VMEM)
    f32 = jnp.float32
    dma = pltpu.SemaphoreType.DMA
    return pl.pallas_call(
        exchange_kernel,
        out_shape=[
            jax.ShapeDtypeStruct((256, 1024), f32),
            jax.ShapeDtypeStruct((NA, 256), f32),
            jax.ShapeDtypeStruct((1, slot), f32),
        ],
        in_specs=[pl.BlockSpec(memory_space=pl.ANY), vmem, vmem],
        out_specs=[vmem] * 3,
        scratch_shapes=[
            pltpu.VMEM((1024, slot), jnp.bfloat16),
            pltpu.VMEM((4, 4, 2, 256, 128), f32),
            pltpu.VMEM((4, 2, 3, 256, 128), f32),
            pltpu.VMEM((4, 2, 256, 128), f32),
            pltpu.VMEM((2, 8, 128, 128), f32),
            pltpu.VMEM((4, 8, 384), f32),
            pltpu.VMEM((4, 3, 8, 384), f32),
            pltpu.VMEM((4, NA, 256), f32),
            pltpu.VMEM((3, NA, 256), f32),
            dma(()),
            dma((16, 2)),
            dma((32,)),
            dma((4, 4, 2)),
            dma((4, 2, 3)),
            dma((4, 2, 2)),
            dma((2, 8)),
            dma((4, 3)),
            dma((4, 3)),
            dma((3,)),
            dma((3,)),
        ],
        compiler_params=pltpu.CompilerParams(collective_id=0, has_side_effects=True, vmem_limit_bytes=44 << 20),
    )(sorted_frames, members, ages)


def local(counts, dark_level, flat_field, valid_pixel, cycle_label, cycle_order, age_bin):
    block_total = dark_level.shape[0] // BLK
    table = (block_total, BLK)
    sorted_frames, member_sums = sort_frames(
        cycle_order[0],
        counts,
        dark_level.reshape(table),
        flat_field.reshape(table),
        valid_pixel.reshape(table),
        cycle_label.reshape(table),
    )
    two_time, aged, image = exchange(sorted_frames, member_sums, age_bin[None, :])
    return (two_time[None], aged[None], image[None])


def solution(mesh):
    in_specs = (
        P("frame", "tile"),
        P("tile"),
        P("tile"),
        P("tile"),
        P("tile"),
        P("tile", None, None),
        P(),
    )
    out_specs = (P("frame", "tile", None), P("frame", None, "tile"), P("tile", "frame", None))
    return jax.shard_map(local, mesh=mesh, in_specs=in_specs, out_specs=out_specs, check_vma=False)
```

time: 225 us -> 168 us (0.75)
  Pallas kernels: 19.1 us -> 160 us
  blocking collectives: 113 us -> 0 us
  waiting for transfers between devices: 46.4 us -> 0 us
  between operations: 14.7 us -> 0.68 us
  other arithmetic: 10.7 us -> 0 us
  matrix products: 10.4 us -> 0 us
  local copies, waits for them, and re-layouts: 9.6 us -> 7.07 us
    pallas_call x1, Pallas kernels: 3.36 us -> 144 us  [exchange(): pl.pallas_call(exchange_kernel, out_shape=[jax.ShapeDtypeStruct((256, 102...]
    all_to_all x1 -> x0, blocking collectives: 99.6 us -> none  [local(): lax.all_to_all(sorted_frames, 'frame', split_axis=0, concat_axis=1, tiled...]
    reduce_scatter x2 -> x0, waiting for transfers between devices: 46.3 us -> none  [the longest x1 26.6 us: local(): gram_rows = lax.psum_scatter(gram, 'tile', scatter_dimension=0, tiled=True)]
    psum x1 -> x0, blocking collectives: 13.2 us -> none  [local(): totals, pixels = lax.psum((cycle_sums, jnp.sum(own)), 'tile')]
    dot_general x1 -> x0, matrix products: 10.4 us -> none  [local(): gram = jnp.dot(exchanged, exchanged.T, preferred_element_type=jnp.float32)]
    reduce_sum x3 -> x0, other arithmetic: 8.57 us -> none  [the longest x1 7.84 us: local(): image = jnp.sum(widened, axis=0) / frames]
    unnamed x16 -> x15, local copies, waits for them, and re-layouts: 9.32 us -> 7.07 us
  transfers between devices with their start and end apart: 2 -> 0, of which waited for: 2 -> 0; matrix products, arithmetic and copies ran while one was open for 4% -> 0% of each run, Pallas kernels for 0% -> 0%
where the time goes in v2:
time: 168 us
  Pallas kernels  160 us (95%)
  local copies, waits for them, and re-layouts  7.07 us (4%)
    pallas_call x1, Pallas kernels, exchange(): pl.pallas_call(exchange_kernel, out_shape=[jax.ShapeDtypeStruct((256, 102...  144 us
    pallas_call x1, Pallas kernels, sort_frames(): pl.pallas_call(sort_kernel, grid_spec=pltpu.PrefetchScalarGridSpec(num_sc...  15.7 us
    unnamed x15, local copies, waits for them, and re-layouts  7.07 us

profile of v2, /device:TPU:18, one launch (start us, length us, event | category | flops | bytes accessed | tf_op | source)
XLA Modules:
  0.0 167.9 jit_solution(15783644962298861240)
XLA Ops:
  0.6 0.0 copy-start.5
  0.6 0.0 copy-start
  0.7 1.0 copy-done
  1.7 0.0 copy-start.1
  1.7 1.0 copy-done.1
  2.7 0.0 copy-start.2
  2.7 1.0 copy-done.2
  3.8 0.0 copy-start.3
  3.8 1.0 copy-done.3
  4.8 0.0 copy-start.4
  4.8 0.7 copy-done.4
  5.5 15.7 %shard_map.94 = (bf16[32,32,4096]{2,1,0:T(8,128)(2,1)S(1)}, f32[32,1,128]{2,1,0:T(1,128)S(1)}) custom-call(s32[32,32]{1,0:T(8,128)S(1)} %bitcast.16, f32[32,131072]{1,0:T(8,128)} %counts.1, f32[1024,128]{1,0:T(8,128)S(1)} %bitcast.10, f32[1024,128]{1,0:T(8,128)S(1)} %bitcast.11, s32[1024,128]{1,0:T(8,128)S(1)} %bitcast.12, s32[1024,128]{1,0:T(8,128)S(1)} %bitcast.13), custom_call_target="tpu_custom_call" | custom-call | flops 12582912 | bytes 25165824 | tf_op jit(solution)/shard_map/pallas_call | solution.py:57
  21.3 0.0 copy-done.5
  21.3 144.4 %shard_map.95 = (f32[256,1024]{1,0:T(8,128)S(1)}, f32[16,256]{1,0:T(8,128)S(1)}, f32[1,4096]{1,0:T(1,128)S(1)}) custom-call(bf16[32,32,4096]{2,1,0:T(8,128)(2,1)S(1)} %get-tuple-element.8.frames_in, f32[32,1,128]{2,1,0:T(1,128)S(1)} %get-tuple-element.9.members, s32[1,1024]{1,0:T(1,128)S(1)} %bitcast.17), custom_call_target="tpu_custom_call" | custom-call | tf_op jit(solution)/shard_map/pallas_call | solution.py:399
  165.8 1.0 copy.13
  166.7 0.6 copy.14
  167.3 0.6 copy.15
Async XLA Ops:
  0.6 20.7 %copy-start.5 = (s32[1024]{0:T(1024)S(1)}, s32[1024]{0:T(1024)}, u32[]{:S(2)}) copy-start(s32[1024]{0:T(1024)} %param.13) | copy-start | bytes 12292
  0.6 1.0 copy-start
  1.7 1.0 copy-start.1
  2.7 1.0 copy-start.2
  3.8 1.0 copy-start.3
  4.8 0.7 copy-start.4

commit v3 on v2

--- a/solution.py
+++ b/solution.py
@@ -7,27 +7,25 @@
 
 BLK = 128
 NA = 16
+AHEAD = 5
 QSTEP = 4
-HALF = 16
+ROWS = 32
 MESH = pl.DeviceIdType.MESH
 
 
 def sort_kernel(order, counts, dark, flat, valid, label, out, sums, held, sem):
-    c, g = pl.program_id(0), pl.program_id(1)
-
-    def load(i):
-        rows = pl.ds(i * HALF, HALF)
-        return pltpu.make_async_copy(counts.at[rows, :], held.at[i], sem.at[i])
-
-    @pl.when((c == 0) & (g == 0))
+    g = pl.program_id(0)
+
+    @pl.when(g == 0)
     def _():
-        load(0).start()
-        load(1).start()
-        load(0).wait()
-
-    @pl.when((c == 1) & (g == 0))
-    def _():
-        load(1).wait()
+        loads = []
+        for r in range(4):
+            rows = pl.ds(8 * r, 8)
+            loads.append(pltpu.make_async_copy(counts.at[rows, :], held.at[rows, :], sem.at[r]))
+        for load in loads:
+            load.start()
+        for load in loads:
+            load.wait()
 
     block_total = dark.shape[0]
     blocks = order.shape[1]
@@ -44,7 +42,7 @@
             usable = jnp.where(label[row, :] == q, valid[row, :].astype(jnp.float32), 0.0) * listed
             total = total + usable
             gain = flat[row, :] * usable
-            columns = held[c, :, pl.ds(pl.multiple_of(at * BLK, BLK), BLK)]
+            columns = held[:, pl.ds(pl.multiple_of(at * BLK, BLK), BLK)]
             out[k, :, b * BLK : (b + 1) * BLK] = ((columns - dark[row, :]) * gain).astype(jnp.bfloat16)
         sums[k] = total
 
@@ -53,20 +51,20 @@
     frames, pixels = counts.shape
     cycles, blocks = block_order.shape
     slot = blocks * BLK
-    table = pl.BlockSpec((pixels // BLK, BLK), lambda c, g, order: (0, 0))
+    table = pl.BlockSpec((pixels // BLK, BLK), lambda g, order: (0, 0))
     return pl.pallas_call(
         sort_kernel,
         grid_spec=pltpu.PrefetchScalarGridSpec(
             num_scalar_prefetch=1,
-            grid=(frames // HALF, cycles // QSTEP),
+            grid=(cycles // QSTEP,),
             in_specs=[pl.BlockSpec(memory_space=pl.ANY), table, table, table, table],
             out_specs=[
-                pl.BlockSpec((QSTEP, HALF, slot), lambda c, g, order: (g, c, 0)),
-                pl.BlockSpec((QSTEP, 1, BLK), lambda c, g, order: (g, 0, 0)),
+                pl.BlockSpec((QSTEP, frames, slot), lambda g, order: (g, 0, 0)),
+                pl.BlockSpec((QSTEP, 1, BLK), lambda g, order: (g, 0, 0)),
             ],
             scratch_shapes=[
-                pltpu.VMEM((frames // HALF, HALF, pixels), jnp.float32),
-                pltpu.SemaphoreType.DMA((frames // HALF,)),
+                pltpu.VMEM((frames, pixels), jnp.float32),
+                pltpu.SemaphoreType.DMA((4,)),
             ],
         ),
         out_shape=[
@@ -74,7 +72,7 @@
             jax.ShapeDtypeStruct((cycles, 1, BLK), jnp.float32),
         ],
         compiler_params=pltpu.CompilerParams(
-            dimension_semantics=("arbitrary", "arbitrary"), vmem_limit_bytes=40 << 20
+            dimension_semantics=("arbitrary",), vmem_limit_bytes=60 << 20
         ),
         cost_estimate=pl.CostEstimate(flops=3 * frames * cycles * slot, bytes_accessed=24 << 20, transcendentals=0),
     )(block_order, counts, dark, flat, valid, label)
@@ -158,11 +156,14 @@
             device_id_type=MESH,
         )
 
-    def quarter():
-        return [(e, h, dc) for first in range(2) for dc in range(2) for e, h in ((0, first), (1, 1 - first))]
-
-    def is_own(k, e, h, dc):
-        return (k, e, h, dc) == (0, 0, 0, 0)
+    def pair(p):
+        k, first = p // 2, p % 2
+        chips = {4: ((1, 0), (0, 1)), 5: ((0, 0), (1, 1))}.get(p, ((0, first), (1, 1 - first)))
+        return [(k, e, h, dc) for dc in range(2) for e, h in chips if (k, e, h, dc) != (0, 0, 0, 0)]
+
+    def send_pair(p):
+        for who in pair(p):
+            send(*who).start()
 
     barrier = pltpu.get_barrier_semaphore()
     for dy in range(4):
@@ -177,14 +178,11 @@
 
     own = pltpu.make_async_copy(frames_in.at[f], frames_of(c), own_sem)
     own.start()
-    for k in range(2):
-        for e, h, dc in quarter():
-            if not is_own(k, e, h, dc):
-                send(k, e, h, dc).start()
+    for p in range(AHEAD):
+        send_pair(p)
 
     ones = jnp.ones((8, 1024), jnp.bfloat16)
-    width = x_all.shape[1]
-    chunks = width // 1024
+    chunks = x_all.shape[1] // 1024
     group = lambda r, j: 4 * (r % 2) + 2 * j + r // 2
 
     def tile_copy(src, dst, send_sem, recv_sem, tile):
@@ -192,75 +190,123 @@
             src_ref=src, dst_ref=dst, send_sem=send_sem, recv_sem=recv_sem, device_id=(f, tile), device_id_type=MESH
         )
 
-    def partial_copy(k, cg, half):
+    def pieces_of(k, cg):
+        if k < 3 or cg == 3:
+            return [(0, 256, 2 * k + 1)]
+        return [(0, 64, 6), (192, 64, 6), (64, 128, 7)]
+
+    def part_send(k, cg, half, i):
         tile = tile_of(cg // 2 + 2 * half)
         slot = 3 - (tile - t + 4) % 4
+        at, n, _ = pieces_of(k, cg)[i]
         return tile, lambda: tile_copy(
-            part.at[k, cg, half],
-            inbox.at[k, cg % 2, slot],
-            ps_sem.at[k, cg, half],
-            pr_sem.at[k, cg % 2, slot],
+            part.at[k, cg, half, pl.ds(at, n), :],
+            inbox.at[k, cg % 2, slot, pl.ds(at, n), :],
+            ps_sem.at[k, cg, half, i],
+            pr_sem.at[k, cg % 2, slot, i],
             tile,
         )
 
-    def share_copy(k, j, e):
+    def start_parts(k, cg, phase):
+        for half in range(2):
+            for i, piece in enumerate(pieces_of(k, cg)):
+                if piece[2] == phase:
+                    tile, copy = part_send(k, cg, half, i)
+
+                    @pl.when(tile != t)
+                    def _():
+                        copy().start()
+
+    def strip(k, cg, phase):
+        rows = [pl.ds(256 * k + at, n) for at, n, when in pieces_of(k, cg) if when == phase]
+        height = sum(n for at, n, when in pieces_of(k, cg) if when == phase)
+
+        def body(i, acc):
+            at = pl.ds(pl.multiple_of(i * 1024, 1024), 1024)
+            new = [x_all[r, at] for r in rows]
+            new = new[0] if len(new) == 1 else jnp.concatenate(new, axis=0)
+            return acc + contract(new, x_all[256 * cg : 256 * cg + 256, at])
+
+        acc = lax.fori_loop(0, chunks, body, jnp.zeros((height, 256), jnp.float32))
+        done = 0
+        for at, n, when in pieces_of(k, cg):
+            if when == phase:
+                for half in range(2):
+                    part[k, cg, half, at : at + n, :] = acc[done : done + n, 128 * half : 128 * half + 128]
+                done += n
+        start_parts(k, cg, phase)
+
+    def segments(k, phase):
+        if k < 3:
+            return [(0, 128), (128, 128)] if phase == 2 * k + 1 else []
+        return [(0, 64), (192, 64)] if phase == 6 else [(64, 64), (128, 64)]
+
+    def share_copy(k, j, at, n):
         g = group(role, j)
+        i = at // 64
         return tile_copy(
-            total.at[k, j, pl.ds(128 * e, 128), :],
-            shared.at[k % 2, g],
-            hs_sem.at[k, j, e],
-            hr_sem.at[k % 2, g],
-            tile_of(k // 2 + 2 * e),
+            total.at[k, j, pl.ds(at, n), :],
+            shared.at[k % 2, g, pl.ds(at % 128, n), :],
+            hs_sem.at[k, j, i],
+            hr_sem.at[k % 2, g, i % 2],
+            tile_of(k // 2 + 2 * (at // 128)),
         )
 
-    def shares_to_wait(k, start):
+    def reduce_parts(k, phase):
         for j in range(2):
-            for e in range(2):
-                for p in range(2):
-                    if 2 * p + j < k:
-
-                        @pl.when((odd == p) & (role != k // 2 + 2 * e))
+            for p in range(2):
+                cg = 2 * p + j
+                pieces = [(i, at, n) for i, (at, n, when) in enumerate(pieces_of(k, cg)) if when == phase]
+                if cg <= k and pieces:
+
+                    @pl.when(odd == p)
+                    def _():
+                        for i, at, n in pieces:
+                            rows = pl.ds(at, n)
+                            for slot in range(3):
+                                tile_copy(
+                                    part.at[k, cg, 0, rows, :],
+                                    inbox.at[k, j, slot, rows, :],
+                                    ps_sem.at[k, cg, 0, i],
+                                    pr_sem.at[k, j, slot, i],
+                                    (t + slot + 1) % 4,
+                                ).wait_recv()
+                            total[k, j, rows, :] = (part[k, cg, side, rows, :] + inbox[k, j, 0, rows, :]) + (
+                                inbox[k, j, 1, rows, :] + inbox[k, j, 2, rows, :]
+                            )
+
+        shares(k, phase, True)
+
+    def shares(k, phase, start):
+        for j in range(2):
+            for p in range(2):
+                if 2 * p + j < k:
+                    for at, n in segments(k, phase):
+                        owner = k // 2 + 2 * (at // 128)
+
+                        @pl.when((odd == p) & (role != owner))
                         def _():
                             if start:
-                                share_copy(k, j, e).start()
+                                share_copy(k, j, at, n).start()
                             else:
-                                share_copy(k, j, e).wait_send()
-
-    for k in range(4):
+                                share_copy(k, j, at, n).wait_send()
+
+                        if start:
+
+                            @pl.when((odd == p) & (role == owner))
+                            def _():
+                                shared[k % 2, group(role, j), at % 128 : at % 128 + n, :] = total[k, j, at : at + n, :]
+
+    def sums_copy(k, dz):
+        return tile_copy(sums.at[k], sums_in.at[k, 3 - dz], ss_sem.at[k, dz - 1], sr_sem.at[k, 3 - dz], (t + dz) % 4)
+
+    def frame_sums(k):
         new = pl.ds(256 * k, 256)
-        for e, h, dc in quarter():
-            if is_own(k, e, h, dc):
-                own.wait()
-            else:
-                arrival(k, e, h, dc).wait_recv()
-        if k < 2:
-            for e, h, dc in quarter():
-                send(k + 2, e, h, dc).start()
-        for cg in range(k + 1):
-
-            def body(i, acc):
-                at = pl.ds(pl.multiple_of(i * 1024, 1024), 1024)
-                return acc + contract(x_all[new, at], x_all[256 * cg : 256 * cg + 256, at])
-
-            acc = lax.fori_loop(0, chunks, body, jnp.zeros((256, 256), jnp.float32))
-            for half in range(2):
-                part[k, cg, half] = acc[:, 128 * half : 128 * half + 128]
-            for half in range(2):
-                tile, copy = partial_copy(k, cg, half)
-
-                @pl.when(tile != t)
-                def _():
-                    copy().start()
-
         line = jnp.zeros((8, 256), jnp.float32)
         for i in range(chunks):
             line = line + contract(ones, x_all[new, i * 1024 : (i + 1) * 1024])
         sums[k, :, 0:256] = line
         sums[k, :, 256:384] = jnp.broadcast_to(members[f], (8, 128))
-        for dz in range(1, 4):
-            tile_copy(
-                sums.at[k], sums_in.at[k, 3 - dz], ss_sem.at[k, dz - 1], sr_sem.at[k, 3 - dz], (t + dz) % 4
-            ).start()
         for i in range(chunks):
             at = slice(i * 1024, (i + 1) * 1024)
             row = jnp.dot(ones[:, 0:256], x_all[new, at], preferred_element_type=jnp.float32)[0:1]
@@ -270,27 +316,27 @@
                 image[:, at] = image[:, at] + row
             else:
                 image[:, at] = (image[:, at] + row) * (1.0 / 1024.0)
-
-        for j in range(2):
-            for p in range(2):
-                cg = 2 * p + j
-                if cg <= k:
-
-                    @pl.when(odd == p)
-                    def _():
-                        for slot in range(3):
-                            tile_copy(
-                                part.at[k, cg, 0], inbox.at[k, j, slot], ps_sem.at[k, cg, 0], pr_sem.at[k, j, slot], (t + slot + 1) % 4
-                            ).wait_recv()
-                        total[k, j] = (part[k, cg, side] + inbox[k, j, 0]) + (inbox[k, j, 1] + inbox[k, j, 2])
-                        if cg < k:
-                            for e in range(2):
-
-                                @pl.when(role == k // 2 + 2 * e)
-                                def _():
-                                    shared[k % 2, group(role, j)] = total[k, j, 128 * e : 128 * e + 128, :]
-
-        shares_to_wait(k, True)
+        for dz in range(1, 4):
+            sums_copy(k, dz).start()
+
+    for p in range(8):
+        k = p // 2
+        for who in pair(p):
+            arrival(*who).wait_recv()
+        if p == 0:
+            own.wait()
+        if p + AHEAD < 8:
+            send_pair(p + AHEAD)
+        for cg in range(k + 1):
+            if any(when == p for at, n, when in pieces_of(k, cg)):
+                strip(k, cg, p)
+        if p % 2 == 0 and p > 0:
+            frame_sums(k - 1)
+            reduce_parts(k - 1, p - 1)
+        if p == 6:
+            reduce_parts(3, 6)
+    frame_sums(3)
+    reduce_parts(3, 7)
 
     for k in range(4):
         for slot in range(3):
@@ -320,9 +366,16 @@
 
                         @pl.when(group(role, g // 2 - 2 * (g // 4)) != g)
                         def _():
-                            tile_copy(
-                                total.at[0, 0, pl.ds(0, 128), :], shared.at[jj, g], hs_sem.at[0, 0, 0], hr_sem.at[jj, g], (t + 1) % 4
-                            ).wait_recv()
+                            n = 64 if kk == 3 else 128
+                            for i in range(128 // n):
+                                rows = pl.ds(i * n, n)
+                                tile_copy(
+                                    total.at[0, 0, rows, :],
+                                    shared.at[jj, g, rows, :],
+                                    hs_sem.at[0, 0, 0],
+                                    hr_sem.at[jj, g, i],
+                                    (t + 1) % 4,
+                                ).wait_recv()
 
                         value = shared[jj, g]
                     else:
@@ -369,23 +422,23 @@
         tile_copy(bands.at[0], bands_in.at[slot], bs_sem.at[0], br_sem.at[slot], (t + slot + 1) % 4).wait_recv()
     aged[...] = ((bands[t] + bands_in[0]) + (bands_in[1] + bands_in[2])) / lag_total
 
+    for p in range(8):
+        for who in pair(p):
+            send(*who).wait_send()
+        for k in range(4):
+            shares(k, p, False) if p == 2 * k + 1 or (k, p) == (3, 6) else None
     for k in range(4):
-        for e, h, dc in quarter():
-            if not is_own(k, e, h, dc):
-                send(k, e, h, dc).wait_send()
         for cg in range(k + 1):
             for half in range(2):
-                tile, copy = partial_copy(k, cg, half)
-
-                @pl.when(tile != t)
-                def _():
-                    copy().wait_send()
+                for i in range(len(pieces_of(k, cg))):
+                    tile, copy = part_send(k, cg, half, i)
+
+                    @pl.when(tile != t)
+                    def _():
+                        copy().wait_send()
 
         for dz in range(1, 4):
-            tile_copy(
-                sums.at[k], sums_in.at[k, 3 - dz], ss_sem.at[k, dz - 1], sr_sem.at[k, 3 - dz], (t + dz) % 4
-            ).wait_send()
-        shares_to_wait(k, False)
+            sums_copy(k, dz).wait_send()
     for dz in range(1, 4):
         peer = (t + dz) % 4
         tile_copy(bands.at[peer], bands_in.at[3 - dz], bs_sem.at[dz - 1], br_sem.at[3 - dz], peer).wait_send()
@@ -418,23 +471,22 @@
             dma(()),
             dma((16, 2)),
             dma((32,)),
-            dma((4, 4, 2)),
-            dma((4, 2, 3)),
-            dma((4, 2, 2)),
-            dma((2, 8)),
+            dma((4, 4, 2, 3)),
+            dma((4, 2, 3, 3)),
+            dma((4, 2, 4)),
+            dma((2, 8, 2)),
             dma((4, 3)),
             dma((4, 3)),
             dma((3,)),
             dma((3,)),
         ],
-        compiler_params=pltpu.CompilerParams(collective_id=0, has_side_effects=True, vmem_limit_bytes=44 << 20),
+        compiler_params=pltpu.CompilerParams(collective_id=0, has_side_effects=True, vmem_limit_bytes=51 << 20),
     )(sorted_frames, members, ages)
 
 
 def local(counts, dark_level, flat_field, valid_pixel, cycle_label, cycle_order, age_bin):
-    block_total = dark_level.shape[0] // BLK
-    table = (block_total, BLK)
-    sorted_frames, member_sums = sort_frames(
+    table = (dark_level.shape[0] // BLK, BLK)
+    sorted_frames, members = sort_frames(
         cycle_order[0],
         counts,
         dark_level.reshape(table),
@@ -442,7 +494,7 @@
         valid_pixel.reshape(table),
         cycle_label.reshape(table),
     )
-    two_time, aged, image = exchange(sorted_frames, member_sums, age_bin[None, :])
+    two_time, aged, image = exchange(sorted_frames, members, age_bin[None, :])
     return (two_time[None], aged[None], image[None])
 
 

time: 168 us -> 159 us (0.946)
  the two profiles are of different devices: /device:TPU:18 before, /device:TPU:11 now
where the time goes in v3:
time: 159 us
  Pallas kernels  155 us (97%)
  local copies, waits for them, and re-layouts  2.9 us (2%)
    pallas_call x1, Pallas kernels, exchange(): pl.pallas_call(exchange_kernel, out_shape=[jax.ShapeDtypeStruct((256, 102...  140 us
    pallas_call x1, Pallas kernels, sort_frames(): pl.pallas_call(sort_kernel, grid_spec=pltpu.PrefetchScalarGridSpec(num_sc...  15.7 us

profile of v3, /device:TPU:11, one launch (start us, length us, event | category | flops | bytes accessed | tf_op | source)
XLA Modules:
  0.0 158.9 jit_solution(16855852545973187029)
XLA Ops:
  0.6 0.0 copy-start.1
  0.6 15.7 %shard_map.94 = (bf16[32,32,4096]{2,1,0:T(8,128)(2,1)}, f32[32,1,128]{2,1,0:T(1,128)}) custom-call(s32[32,32]{1,0:T(8,128)} %bitcast.17, f32[32,131072]{1,0:T(8,128)} %counts.1, f32[1024,128]{1,0:T(8,128)} %bitcast.13, f32[1024,128]{1,0:T(8,128)} %bitcast.14, s32[1024,128]{1,0:T(8,128)} %bitcast.15, s32[1024,128]{1,0:T(8,128)} %bitcast.16), custom_call_target="tpu_custom_call" | custom-call | flops 12582912 | bytes 25165824 | tf_op jit(solution)/shard_map/pallas_call | solution.py:55
  16.4 0.0 copy-done.1
  16.4 0.0 copy-start
  16.4 0.7 copy-done
  17.1 139.6 %shard_map.95 = (f32[256,1024]{1,0:T(8,128)S(1)}, f32[16,256]{1,0:T(8,128)S(1)}, f32[1,4096]{1,0:T(1,128)S(1)}) custom-call(bf16[32,32,4096]{2,1,0:T(8,128)(2,1)} %get-tuple-element.8.frames_in, f32[32,1,128]{2,1,0:T(1,128)S(1)} %copy-done, s32[1,1024]{1,0:T(1,128)S(1)} %bitcast.12), custom_call_target="tpu_custom_call" | custom-call | tf_op jit(solution)/shard_map/pallas_call | solution.py:452
  156.7 1.0 copy.13
  157.7 0.6 copy.14
  158.3 0.6 copy.15
Async XLA Ops:
  0.6 15.7 %copy-start.1 = (s32[1024]{0:T(1024)S(1)}, s32[1024]{0:T(1024)}, u32[]{:S(2)}) copy-start(s32[1024]{0:T(1024)} %param.13) | copy-start | bytes 12292
  16.4 0.7 copy-start
